TPU v7x, 128 devices: a whole 4x4x4 slice. The times are simulated.
128 devices in a mesh: space: 16 (over y_hi, x, core), code: 4 (over z), clip: 2 (over y_lo).
Axes of the slice: x: 4, y: 4 (y_hi: 2, y_lo: 2; y = y_hi * 2 + y_lo), z: 4, core: 2. Of those that a mesh axis runs over, the one named last changes fastest.
Arguments:
- soft_weights: bfloat16 [2, 1024, 32, 8192], P('clip', 'space', None, 'code'), may hold values from 0.00029945374 to 0.029907227
- codebook: bfloat16 [8192, 256], P('code'), may hold values from -6 to 6
- kernel_one: bfloat16 [3, 3, 256, 512], replicated, may hold values from -0.125 to 0.125
- kernel_two: bfloat16 [3, 3, 512, 512], replicated, may hold values from -0.09375 to 0.09375
- cotangent: bfloat16 [2, 1024, 32, 512], P('clip', ('space', 'code')), may hold values from -16 to 16
Outputs:
- decoded: bfloat16 [2, 1024, 32, 512], P('clip', ('space', 'code'))
- grad_one: float32 [3, 3, 256, 512], P(None, None, None, ('space', 'code', 'clip'))
- grad_two: float32 [3, 3, 512, 512], P(None, None, None, ('space', 'code', 'clip'))
- grad_codebook: float32 [8192, 256], P('code')
All inputs are finite; a program needn't handle non-finite values.
Results may differ from a plain program's by a relative error of at most 0.02.
Values may be sent and summed in bfloat16 or wider, within the bound.
A program may use at most 192 MiB of HBM per device.

v0:
```python
import jax
import jax.numpy as jnp
from jax import lax
from jax.sharding import PartitionSpec as P


def with_halo(block, sides, width):
    for axis, dim in sides:
        count = lax.axis_size(axis)
        forward = [(i, i + 1) for i in range(count - 1)]
        backward = [(target, source) for source, target in forward]
        low = lax.ppermute(
            lax.slice_in_dim(block, block.shape[dim] - width, None, axis=dim), axis, forward
        )
        high = lax.ppermute(lax.slice_in_dim(block, 0, width, axis=dim), axis, backward)
        block = jnp.concatenate([low, block, high], axis=dim)
    return block


def extend(field):
    grown = with_halo(field, ((("space", "code"), 0),), 1)
    return jnp.pad(grown, ((0, 0), (1, 1), (0, 0)))


def taps_forward(padded, kernel):
    height = padded.shape[0] - 2
    breadth = padded.shape[1] - 2
    accum = jnp.zeros((height * breadth, kernel.shape[3]), jnp.float32)
    for first in range(3):
        for second in range(3):
            window = padded[first : first + height, second : second + breadth].reshape(
                height * breadth, -1
            )
            accum = accum + jnp.dot(
                window, kernel[first, second], preferred_element_type=jnp.float32
            )
    return accum.reshape(height, breadth, -1)


def taps_back(padded, kernel):
    height = padded.shape[0] - 2
    breadth = padded.shape[1] - 2
    accum = jnp.zeros((height * breadth, kernel.shape[2]), jnp.float32)
    for first in range(3):
        for second in range(3):
            window = padded[
                2 - first : 2 - first + height, 2 - second : 2 - second + breadth
            ].reshape(height * breadth, -1)
            accum = accum + jnp.dot(
                window, kernel[first, second].T, preferred_element_type=jnp.float32
            )
    return accum.reshape(height, breadth, -1)


def kernel_grad(padded, upstream):
    height = upstream.shape[0]
    breadth = upstream.shape[1]
    flat_up = upstream.reshape(height * breadth, -1)
    result = []
    for first in range(3):
        line = []
        for second in range(3):
            window = padded[first : first + height, second : second + breadth].reshape(
                height * breadth, -1
            )
            line.append(
                lax.dot_general(
                    window, flat_up, (((0,), (0,)), ((), ())), preferred_element_type=jnp.float32
                )
            )
        result.append(jnp.stack(line))
    return jnp.stack(result)


def on_device(soft_weights, codebook, kernel_one, kernel_two, cotangent):
    weights = soft_weights[0]
    upstream = cotangent[0]
    own_rows = upstream.shape[0]
    breadth = weights.shape[1]
    code_slice = weights.shape[2]
    partial_value = jnp.dot(
        weights.reshape(-1, code_slice), codebook, preferred_element_type=jnp.float32
    )
    partial_value = partial_value.reshape(weights.shape[0], breadth, -1)
    summed = lax.psum(partial_value, "code")
    owned = lax.dynamic_slice_in_dim(summed, lax.axis_index("code") * own_rows, own_rows, 0)
    embedded = owned.astype(jnp.bfloat16)
    embed_pad = extend(embedded)
    pre_one = taps_forward(embed_pad, kernel_one)
    hidden = jax.nn.silu(pre_one).astype(jnp.bfloat16)
    hidden_pad = extend(hidden)
    decoded = taps_forward(hidden_pad, kernel_two).astype(jnp.bfloat16)
    grad_hidden = taps_back(extend(upstream), kernel_two)
    sigma = jax.nn.sigmoid(pre_one)
    grad_pre = (grad_hidden * sigma * (1.0 + pre_one * (1.0 - sigma))).astype(jnp.bfloat16)
    grad_embedded = taps_back(extend(grad_pre), kernel_one).astype(jnp.bfloat16)
    piece = lax.all_gather(grad_embedded, "code", axis=0, tiled=True)
    code_terms = lax.dot_general(
        weights.reshape(-1, code_slice),
        piece.reshape(-1, piece.shape[2]),
        (((0,), (0,)), ((), ())),
        preferred_element_type=jnp.float32,
    )
    grad_codebook = lax.psum(code_terms.astype(jnp.bfloat16), ("space", "clip")).astype(jnp.float32)
    term_two = kernel_grad(hidden_pad, upstream)
    term_one = kernel_grad(embed_pad, grad_pre)
    grad_one, grad_two = (
        lax.psum_scatter(term_one, ("space", "code", "clip"), scatter_dimension=3, tiled=True),
        lax.psum_scatter(term_two, ("space", "code", "clip"), scatter_dimension=3, tiled=True),
    )
    return (decoded[None], grad_one, grad_two, grad_codebook)


def solution(mesh):
    in_specs = (
        P("clip", "space", None, "code"),
        P("code", None),
        P(),
        P(),
        P("clip", ("space", "code"), None, None),
    )
    out_specs = (
        P("clip", ("space", "code"), None, None),
        P(None, None, None, ("space", "code", "clip")),
        P(None, None, None, ("space", "code", "clip")),
        P("code", None),
    )
    return jax.shard_map(
        on_device, mesh=mesh, in_specs=in_specs, out_specs=out_specs, check_vma=False
    )
```

profile of v0, /device:TPU:1, one launch (start us, length us, event | category | flops | bytes accessed | tf_op | source)
XLA Modules:
  0.0 509.3 jit_solution(13997313864569233537)
XLA Ops:
  8.4 5.7 %fusion = f32[64,32,256]{2,1,0:T(8,128)S(1)} fusion(bf16[1,64,32,2048]{3,2,1,0:T(8,128)(2,1)} %param.5, bf16[2048,256]{1,0:T(8,128)(2,1)S(1)} %copy-done), kind=kOutput, calls=%fused_computation.1 | convolution fusion | flops 2147483648 | bytes 11534336 | tf_op jit(solution)/shard_map/dot_general | solution.py:81
  14.1 44.1 %all-reduce.14 = bf16[64,32,256]{2,1,0:T(8,128)(2,1)} all-reduce(f32[64,32,256]{2,1,0:T(8,128)S(1)} %fusion), channel_id=1, replica_groups=mesh['space'=16,'code'=4,'clip'=2] {'code'}, use_global_device_ids=true, to_apply=%region_0.0 | all-reduce | flops 524288 | bytes 3145728 | tf_op jit(solution)/shard_map/psum | solution.py:85
  59.4 1.9 collective-permute-start
  61.3 5.2 %collective-permute-start.1 = (bf16[1,32,256]{2,1,0:T(8,128)(2,1)S(1)}, bf16[1,32,256]{2,1,0:T(8,128)(2,1)S(1)}, u32[]{:S(2)}, u32[]{:S(2)}) collective-permute-start(bf16[1,32,256]{2,1,0:T(8,128)(2,1)S(1)} %get-tuple-element.55), channel_id=1, source_target_pairs={{2,0},{4,2},{6,4},{8,6},{10,8},{12,10},{14,12},{16,14},{18,16},{20... | collective-permute-start | bytes 49160 | tf_op jit(solution)/shard_map/ppermute | solution.py:15
  66.5 1.9 collective-permute-start.4
  68.5 4.9 collective-permute-start.5
  88.3 1.9 collective-permute-start.2
  90.2 4.9 collective-permute-start.3
  95.0 1.9 collective-permute-start.6
  97.0 5.0 collective-permute-start.7
  103.2 2.7 pad_maximum_fusion.1
  105.8 7.3 %copy.12 = f32[3,3,256,512]{2,1,0,3:T(4,128)} copy(f32[3,3,256,512]{3,2,1,0:T(8,128)} %pad_maximum_fusion.1) | data formatting | bytes 9437184 | tf_op jit(solution)/shard_map/stack | solution.py:72
  113.4 2.0 fusion.114
  127.8 3.4 maximum_bitcast_fusion
  131.2 27.6 %all-gather.2.cloned.1.call-done = bf16[64,32,256]{2,1,0:T(8,128)(2,1)} async-done(((bf16[16,32,256]{2,1,0:T(8,128)(2,1)}), bf16[64,32,256]{2,1,0:T(8,128)(2,1)}) %all-gather.2.cloned.1.call-update) | async-done | bytes 1048592 | tf_op jit(solution)/shard_map/all_gather | solution.py:97
  158.8 7.0 %fusion.2 = bf16[2048,256]{0,1:T(8,128)(2,1)} fusion(bf16[2048,256]{1,0:T(8,128)(2,1)} %bitcast.297, bf16[2048,2048]{1,0:T(8,128)(2,1)} %bitcast.275), kind=kOutput, calls=%fused_computation.8 | convolution fusion | flops 2148007936 | bytes 10485760 | tf_op jit(solution)/shard_map/dot_general | solution.py:98
  166.1 2.3 maximum_bitcast_fusion.2
  169.9 4.7 pad_maximum_fusion
  174.6 13.8 %copy.13 = f32[3,3,512,512]{2,1,0,3:T(4,128)} copy(f32[3,3,512,512]{3,2,1,0:T(8,128)} %pad_maximum_fusion) | data formatting | bytes 18874368 | tf_op jit(solution)/shard_map/stack | solution.py:72
  188.5 1.7 fusion.32
  200.8 2.4 fusion.7
  203.2 70.1 %all-reduce.11.cloned.1.call-done = bf16[2048,256]{0,1:T(8,128)(2,1)} async-done(((bf16[2048,256]{0,1:T(8,128)(2,1)}), bf16[2048,256]{0,1:T(8,128)(2,1)}) %all-reduce.11.cloned.1.call-update) | async-done | bytes 1048592 | tf_op jit(solution)/shard_map/psum | solution.py:104
  273.2 2.6 copy.16
  275.8 223.9 %all-reduce.13.cloned.1.call-done = (f32[3,3,256,512]{2,1,0,3:T(4,128)}, f32[3,3,512,512]{2,1,0,3:T(4,128)}) async-done(((f32[3,3,256,512]{2,1,0,3:T(4,128)}, f32[3,3,512,512]{2,1,0,3:T(4,128)}), (f32[3,3,256,512]{2,1,0,3:T(4,128)}, f32[3,3,512,512]{2,1,0,3:T(4,128)})) %all-reduce.13.cloned.1.call-update) | async-done | bytes 14155792
  (144 shorter events, 45.8 us)
Async XLA Ops:
  7.2 151.6 %all-gather.2.cloned.1.call-start = ((), (), s32[]{:S(2)}) async-start(), calls=%async_computation | async-start | bytes 1310720 | tf_op jit(solution)/shard_map/all_gather | solution.py:97
  14.1 52.4 %copy-start.2 = (bf16[1,16,32,512]{3,2,1,0:T(8,128)(2,1)S(1)}, bf16[1,16,32,512]{3,2,1,0:T(8,128)(2,1)}, u32[]{:S(2)}) copy-start(bf16[1,16,32,512]{3,2,1,0:T(8,128)(2,1)} %param.9) | copy-start | bytes 1572868
  58.3 15.5 %copy-start.5 = (bf16[3,3,256,512]{3,2,1,0:T(8,128)(2,1)S(1)}, bf16[3,3,256,512]{3,2,1,0:T(8,128)(2,1)}, u32[]{:S(2)}) copy-start(bf16[3,3,256,512]{3,2,1,0:T(8,128)(2,1)} %param.7) | copy-start | bytes 7077892
  59.4 13.9 %collective-permute-start = (bf16[1,32,256]{2,1,0:T(8,128)(2,1)S(1)}, bf16[1,32,256]{2,1,0:T(8,128)(2,1)S(1)}, u32[]{:S(2)}, u32[]{:S(2)}) collective-permute-start(bf16[1,32,256]{2,1,0:T(8,128)(2,1)S(1)} %get-tuple-element.54), channel_id=1, source_target_pairs={{0,2},{2,4},{4,6},{6,8},{8,10},{10,12},{12,14},{14,16},{16,18},{18... | collective-permute-start | bytes 49160 | tf_op jit(solution)/shard_map/ppermute | solution.py:12
  61.3 12.0 %collective-permute-start.1 = (bf16[1,32,256]{2,1,0:T(8,128)(2,1)S(1)}, bf16[1,32,256]{2,1,0:T(8,128)(2,1)S(1)}, u32[]{:S(2)}, u32[]{:S(2)}) collective-permute-start(bf16[1,32,256]{2,1,0:T(8,128)(2,1)S(1)} %get-tuple-element.55), channel_id=1, source_target_pairs={{2,0},{4,2},{6,4},{8,6},{10,8},{12,10},{14,12},{16,14},{18,16},{20... | collective-permute-start | bytes 49160 | tf_op jit(solution)/shard_map/ppermute | solution.py:15
  66.5 11.5 %collective-permute-start.4 = (bf16[1,32,512]{2,1,0:T(8,128)(2,1)S(1)}, bf16[1,32,512]{2,1,0:T(8,128)(2,1)S(1)}, u32[]{:S(2)}, u32[]{:S(2)}) collective-permute-start(bf16[1,32,512]{2,1,0:T(8,128)(2,1)S(1)} %get-tuple-element.40), channel_id=1, source_target_pairs={{0,2},{2,4},{4,6},{6,8},{8,10},{10,12},{12,14},{14,16},{16,18},{18... | collective-permute-start | bytes 98312 | tf_op jit(solution)/shard_map/ppermute | solution.py:12
  68.5 9.6 %collective-permute-start.5 = (bf16[1,32,512]{2,1,0:T(8,128)(2,1)S(1)}, bf16[1,32,512]{2,1,0:T(8,128)(2,1)S(1)}, u32[]{:S(2)}, u32[]{:S(2)}) collective-permute-start(bf16[1,32,512]{2,1,0:T(8,128)(2,1)S(1)} %get-tuple-element.41), channel_id=1, source_target_pairs={{2,0},{4,2},{6,4},{8,6},{10,8},{12,10},{14,12},{16,14},{18,16},{20... | collective-permute-start | bytes 98312 | tf_op jit(solution)/shard_map/ppermute | solution.py:15
  76.5 7.6 %copy-start.19 = (f32[512,512]{1,0:T(8,128)}, f32[512,512]{1,0:T(8,128)S(1)}, u32[]{:S(2)}) copy-start(f32[512,512]{1,0:T(8,128)S(1)} %fusion.6) | copy-start | bytes 3145732
  76.5 2.9 slice-start
  84.6 3.0 copy-start.6
  84.6 17.8 %copy-start.8 = (bf16[16,32,512]{2,1,0:T(8,128)(2,1)}, bf16[16,32,512]{2,1,0:T(8,128)(2,1)S(1)}, u32[]{:S(2)}) copy-start(bf16[16,32,512]{2,1,0:T(8,128)(2,1)S(1)} %get-tuple-element.14) | copy-start | bytes 1572868
  88.3 24.8 %collective-permute-start.2 = (bf16[1,32,512]{2,1,0:T(8,128)(2,1)}, bf16[1,32,512]{2,1,0:T(8,128)(2,1)S(1)}, u32[]{:S(2)}, u32[]{:S(2)}) collective-permute-start(bf16[1,32,512]{2,1,0:T(8,128)(2,1)} %get-tuple-element.44), channel_id=1, source_target_pairs={{0,2},{2,4},{4,6},{6,8},{8,10},{10,12},{12,14},{14,16},{16,18},{18... | collective-permute-start | bytes 98312 | tf_op jit(solution)/shard_map/ppermute | solution.py:12
  90.2 22.9 %collective-permute-start.3 = (bf16[1,32,512]{2,1,0:T(8,128)(2,1)}, bf16[1,32,512]{2,1,0:T(8,128)(2,1)S(1)}, u32[]{:S(2)}, u32[]{:S(2)}) collective-permute-start(bf16[1,32,512]{2,1,0:T(8,128)(2,1)} %get-tuple-element.45), channel_id=1, source_target_pairs={{2,0},{4,2},{6,4},{8,6},{10,8},{12,10},{14,12},{16,14},{18,16},{20... | collective-permute-start | bytes 98312 | tf_op jit(solution)/shard_map/ppermute | solution.py:15
  95.0 20.3 %collective-permute-start.6 = (bf16[1,32,512]{2,1,0:T(8,128)(2,1)}, bf16[1,32,512]{2,1,0:T(8,128)(2,1)S(1)}, u32[]{:S(2)}, u32[]{:S(2)}) collective-permute-start(bf16[1,32,512]{2,1,0:T(8,128)(2,1)} %get-tuple-element.36), channel_id=1, source_target_pairs={{0,2},{2,4},{4,6},{6,8},{8,10},{10,12},{12,14},{14,16},{16,18},{18... | collective-permute-start | bytes 98312 | tf_op jit(solution)/shard_map/ppermute | solution.py:12
  97.0 18.4 %collective-permute-start.7 = (bf16[1,32,512]{2,1,0:T(8,128)(2,1)}, bf16[1,32,512]{2,1,0:T(8,128)(2,1)S(1)}, u32[]{:S(2)}, u32[]{:S(2)}) collective-permute-start(bf16[1,32,512]{2,1,0:T(8,128)(2,1)} %get-tuple-element.37), channel_id=1, source_target_pairs={{2,0},{4,2},{6,4},{8,6},{10,8},{12,10},{14,12},{16,14},{18,16},{20... | collective-permute-start | bytes 98312 | tf_op jit(solution)/shard_map/ppermute | solution.py:15
  105.8 7.3 %copy-start.7 = (bf16[16,32,512]{2,1,0:T(8,128)(2,1)S(1)}, bf16[16,32,512]{2,1,0:T(8,128)(2,1)}, u32[]{:S(2)}) copy-start(bf16[16,32,512]{2,1,0:T(8,128)(2,1)} %copy-done.6) | copy-start | bytes 1572868
  120.8 152.5 %all-reduce.11.cloned.1.call-start = ((), (), s32[]{:S(2)}) async-start(), calls=%async_computation.1 | async-start | bytes 2097152 | tf_op jit(solution)/shard_map/psum | solution.py:104
  120.9 2.4 copy-start.17
  125.7 2.0 copy-start.24
  165.8 333.9 %all-reduce.13.cloned.1.call-start = ((), (), s32[]{:S(2)}) async-start(), calls=%async_computation.2 | async-start | bytes 37748736
  166.1 2.8 copy-start.3
  166.1 3.8 copy-start.4
  188.5 3.2 copy-start.18
  200.8 302.0 %copy-start.1 = (bf16[2048,256]{1,0:T(8,128)(2,1)S(1)}, bf16[2048,256]{1,0:T(8,128)(2,1)}, u32[]{:S(2)}) copy-start(bf16[2048,256]{1,0:T(8,128)(2,1)} %param.6) | copy-start | bytes 3145732
  (14 other events, 22.5 us)
Sparse Core Ops, SparseCore 0:
  120.9 37.8 all-gather.1
  166.0 107.2 all-reduce.10
  278.8 220.8 all-reduce.12
where the time goes:
time: 511 us; the launch traced here: 509 us
  waiting for transfers between devices  322 us (63%)
  matrix products  49.1 us (10%)
  blocking collectives  44.1 us (9%)
  local copies, waits for them, and re-layouts  36.6 us (7%)
  starting transfers between devices  27.9 us (5%)
  other arithmetic  15.2 us (3%)
  between operations  14.6 us (3%)
    unnamed x4, waiting for transfers between devices  224 us
    psum x1, waiting for transfers between devices, on_device(): lax.psum(code_terms.astype(jnp.bfloat16), ('space', 'clip'))  70.1 us
    psum x1, blocking collectives, on_device(): summed = lax.psum(partial_value, 'code')  44.1 us
    all_gather x1, waiting for transfers between devices, on_device(): piece = lax.all_gather(grad_embedded, 'code', axis=0, tiled=True)  27.6 us
    another operation x2, local copies, waits for them, and re-layouts, kernel_grad(): return jnp.stack(result)  21.1 us
    ppermute x4, starting transfers between devices, with_halo(): lax.ppermute(lax.slice_in_dim(block, 0, width, axis=dim), axis, backward)  19.9 us
    dot_general x18, matrix products, taps_forward(): jnp.dot(window, kernel[first, second], preferred_element_type=jnp.float32)  17.2 us
    another operation x6, other arithmetic, kernel_grad(): return jnp.stack(result)  13.6 us
  transfers between devices with their start and end apart: 11, of which 3 were waited for; matrix products, arithmetic and copies ran while one was open for 13% of the time, Pallas kernels for 0%

commit v1 on v0

v1 whole, which is shorter than its diff:
```python
import functools

import jax
import jax.numpy as jnp
from jax import lax
from jax.experimental import pallas as pl
from jax.experimental.pallas import tpu as pltpu
from jax.sharding import PartitionSpec as P

MESH = pl.DeviceIdType.MESH
F32 = jnp.float32
BF16 = jnp.bfloat16
COLS = 32
COLOURS = 6


def dot(a, b):
    return jnp.dot(a, b, preferred_element_type=F32)


def dot_nt(a, b):
    return lax.dot_general(a, b, (((1,), (1,)), ((), ())), preferred_element_type=F32)


def rem(a, b):
    return lax.rem(a, jnp.int32(b))


def div(a, b):
    return lax.div(a, jnp.int32(b))


def coords():
    space = lax.axis_index("space")
    return {
        "core": rem(space, 2),
        "x": rem(div(space, 2), 4),
        "y_hi": div(space, 8),
        "z": lax.axis_index("code"),
        "y_lo": lax.axis_index("clip"),
    }


def device(here, **moved):
    at = dict(here, **moved)
    return {
        "space": at["y_hi"] * 8 + at["x"] * 2 + at["core"],
        "code": at["z"],
        "clip": at["y_lo"],
    }


def flip(value):
    return value + 1 - 2 * rem(value, 2)


def links(here):
    y = here["y_hi"] * 2 + here["y_lo"]
    partners = [
        device(here, x=flip(here["x"])),
        device(here, x=3 - here["x"]),
        device(here, y_lo=1 - here["y_lo"]),
        device(here, y_hi=1 - here["y_hi"], y_lo=1 - here["y_lo"]),
        device(here, z=flip(here["z"])),
        device(here, z=3 - here["z"]),
    ]
    bits = []
    for at in (here["x"], y, here["z"]):
        bits += [rem(at + div(at, 2), 2), div(at, 2)]
    return partners, bits


class Wire:
    def __init__(self, send_sems, recv_sems):
        self.send_sems = send_sems
        self.recv_sems = recv_sems
        self.count = 0
        self.sent = []

    def copy(self, src, dst, to):
        made = pltpu.make_async_remote_copy(
            src_ref=src,
            dst_ref=dst,
            send_sem=self.send_sems.at[self.count],
            recv_sem=self.recv_sems.at[self.count],
            device_id=to,
            device_id_type=MESH,
        )
        self.count += 1
        made.start()
        self.sent.append(made)
        return made

    def drain(self):
        for made in self.sent:
            made.wait_send()


def greet(devices):
    barrier = pltpu.get_barrier_semaphore()
    for to in devices:
        pl.semaphore_signal(barrier, inc=1, device_id=to, device_id_type=MESH)
    pl.semaphore_wait(barrier, len(devices))


def front_kernel(
    w_hbm, book, cot, ext_e, ext_c,
    wbuf, keep_u, keep_v, keep_own, snd_a, snd_b, rcv_a, rcv_b, own, halo_e, halo_c,
    load_sem, send_sems, recv_sems,
):
    here = coords()
    z = here["z"]
    block = lax.axis_index("space") * 4 + z
    blocks = lax.axis_size("space") * 4
    cells = own.shape[0]
    half = book.shape[1] // 2
    edge = 2 * COLS
    zu, zv = flip(z), 3 - z
    order = [rem(z + 2, 4), zu, zv, z]
    loads = []
    for slot, chunk in enumerate(order):
        rows = pl.ds(pl.multiple_of(chunk * cells, cells), cells)
        load = pltpu.make_async_copy(w_hbm.at[rows], wbuf.at[slot], load_sem.at[slot])
        load.start()
        loads.append(load)

    def at_block(index):
        return {"space": div(index, 4), "code": rem(index, 4)}

    after, before = at_block(rem(block + 1, blocks)), at_block(rem(block + blocks - 1, blocks))
    to_u, to_v = device(here, z=zu), device(here, z=zv)
    greet([to_u, to_v, after, before])
    wire = Wire(send_sems, recv_sems)
    cot_down = wire.copy(cot.at[pl.ds(cells - edge, edge)], halo_c.at[0], after)
    cot_up = wire.copy(cot.at[pl.ds(0, edge)], halo_c.at[1], before)

    def partial(slot):
        loads[slot].wait()
        return dot(wbuf[slot], book[...])

    value = partial(0)
    snd_a[1] = value[:, :half].astype(BF16)
    snd_b[1] = value[:, half:].astype(BF16)
    far_a = wire.copy(snd_a.at[1], rcv_a.at[1], to_u)
    far_b = wire.copy(snd_b.at[1], rcv_b.at[1], to_v)
    value = partial(1)
    snd_a[0] = value[:, :half].astype(BF16)
    near_a = wire.copy(snd_a.at[0], rcv_a.at[0], to_u)
    keep_u[...] = value[:, half:]
    value = partial(2)
    snd_b[0] = value[:, half:].astype(BF16)
    near_b = wire.copy(snd_b.at[0], rcv_b.at[0], to_v)
    keep_v[...] = value[:, :half]
    keep_own[...] = partial(3)
    far_a.wait_recv()
    snd_a[2] = (keep_v[...] + rcv_a[1].astype(F32)).astype(BF16)
    last_a = wire.copy(snd_a.at[2], rcv_a.at[2], to_v)
    far_b.wait_recv()
    snd_b[2] = (keep_u[...] + rcv_b[1].astype(F32)).astype(BF16)
    last_b = wire.copy(snd_b.at[2], rcv_b.at[2], to_u)
    cot_down.wait_recv()
    cot_up.wait_recv()
    zero_c = jnp.zeros((edge, cot.shape[1]), BF16)
    ext_c[pl.ds(0, edge)] = jnp.where(block == 0, zero_c, halo_c[0])
    ext_c[pl.ds(edge, cells)] = cot[...]
    ext_c[pl.ds(edge + cells, edge)] = jnp.where(block == blocks - 1, zero_c, halo_c[1])
    near_a.wait_recv()
    near_b.wait_recv()
    last_a.wait_recv()
    own[:, :half] = (
        keep_own[:, :half] + rcv_a[0].astype(F32) + rcv_a[2].astype(F32)
    ).astype(BF16)
    last_b.wait_recv()
    own[:, half:] = (
        keep_own[:, half:] + rcv_b[0].astype(F32) + rcv_b[2].astype(F32)
    ).astype(BF16)
    down = wire.copy(own.at[pl.ds(cells - edge, edge)], halo_e.at[0], after)
    up = wire.copy(own.at[pl.ds(0, edge)], halo_e.at[1], before)
    ext_e[pl.ds(edge, cells)] = own[...]
    down.wait_recv()
    up.wait_recv()
    zero_e = jnp.zeros((edge, book.shape[1]), BF16)
    ext_e[pl.ds(0, edge)] = jnp.where(block == 0, zero_e, halo_e[0])
    ext_e[pl.ds(edge + cells, edge)] = jnp.where(block == blocks - 1, zero_e, halo_e[1])
    wire.drain()


def front(weights, codebook, cotangent):
    cells, chan = cotangent.shape[0], codebook.shape[1]
    wide = cotangent.shape[1]
    half = chan // 2
    long = cells + 4 * COLS
    vmem = pl.BlockSpec(memory_space=pltpu.VMEM)
    return pl.pallas_call(
        front_kernel,
        out_shape=(
            jax.ShapeDtypeStruct((long, chan), BF16),
            jax.ShapeDtypeStruct((long, wide), BF16),
        ),
        in_specs=[pl.BlockSpec(memory_space=pl.ANY), vmem, vmem],
        out_specs=(vmem, vmem),
        scratch_shapes=[
            pltpu.VMEM((4, cells, weights.shape[1]), BF16),
            pltpu.VMEM((cells, half), F32),
            pltpu.VMEM((cells, half), F32),
            pltpu.VMEM((cells, chan), F32),
            pltpu.VMEM((3, cells, half), BF16),
            pltpu.VMEM((3, cells, half), BF16),
            pltpu.VMEM((3, cells, half), BF16),
            pltpu.VMEM((3, cells, half), BF16),
            pltpu.VMEM((cells, chan), BF16),
            pltpu.VMEM((2, 2 * COLS, chan), BF16),
            pltpu.VMEM((2, 2 * COLS, wide), BF16),
            pltpu.SemaphoreType.DMA((4,)),
            pltpu.SemaphoreType.DMA((10,)),
            pltpu.SemaphoreType.DMA((10,)),
        ],
        compiler_params=pltpu.CompilerParams(collective_id=0, has_side_effects=True),
        name="front",
    )(weights, codebook, cotangent)


def shifted(value, out):
    rows, chan = value.shape
    column = lax.broadcasted_iota(jnp.int32, (rows, chan), 0) & (COLS - 1)
    wide = value.astype(F32)
    zero = jnp.zeros_like(wide)
    out[:, :chan] = jnp.where(column == 0, zero, pltpu.roll(wide, 1, 0)).astype(BF16)
    out[:, chan : 2 * chan] = value.astype(BF16)
    out[:, 2 * chan :] = jnp.where(
        column == COLS - 1, zero, pltpu.roll(wide, rows - 1, 0)
    ).astype(BF16)


def permuted_rows(colour, size):
    row = lax.broadcasted_iota(jnp.int32, (size, 128), 0)
    bit = {}
    for step in range(6):
        bit[(colour + step) % 6] = (row >> (7 - step)) & 1
    core = row >> 8
    x = bit[1] * 2 + (bit[0] ^ bit[1])
    y_hi, y_lo = bit[3], bit[2] ^ bit[3]
    z = bit[5] * 2 + (bit[4] ^ bit[5])
    channel = y_hi * 256 + x * 64 + core * 32 + z * 8 + y_lo * 4 + (row & 3)
    lane = lax.broadcasted_iota(jnp.int32, (size, 128), 1)
    shift = channel - lane
    return jnp.concatenate(
        [(shift == part * 128).astype(F32).astype(BF16) for part in range(size // 128)], axis=1
    )


def segments(colour, start, width, span):
    found = []
    at, stop = (colour - start) * span, (colour - start + 1) * span
    while at < stop:
        tap = at // width
        end = min(stop, (tap + 1) * width)
        found.append((tap, at - tap * width, end - tap * width))
        at = end
    return found


def local_kernel(
    ext_e, ext_c, k_one, k_two, decoded, grad_e, terms,
    e_cat, c_cat, h_cat, g_cat, pre, grad_pre, left,
):
    block = lax.axis_index("space") * 4 + lax.axis_index("code")
    blocks = lax.axis_size("space") * 4
    cells, wide = decoded.shape
    chan = ext_e.shape[1]
    more = cells + 2 * COLS
    span = terms.shape[3]
    shifted(ext_e[...], e_cat)
    shifted(ext_c[...], c_cat)
    value = dot(e_cat[pl.ds(0, more)], k_one[0])
    for tap in (1, 2):
        value += dot(e_cat[pl.ds(tap * COLS, more)], k_one[tap])
    pre[...] = value
    row = lax.broadcasted_iota(jnp.int32, (more, wide), 0)
    outside = ((row < COLS) & (block == 0)) | ((row >= more - COLS) & (block == blocks - 1))
    sigma = 1.0 / (1.0 + jnp.exp(-value))
    shifted(jnp.where(outside, 0.0, value * sigma).astype(BF16), h_cat)
    value = jnp.zeros((more, wide), F32)
    for a in range(3):
        for b in range(3):
            piece = c_cat[pl.ds((2 - a) * COLS, more), pl.ds((2 - b) * wide, wide)]
            value += dot_nt(piece, k_two[a, pl.ds(b * wide, wide)])
    sigma = 1.0 / (1.0 + jnp.exp(-pre[...]))
    value = value * sigma * (1.0 + pre[...] * (1.0 - sigma))
    value = jnp.where(outside, 0.0, value).astype(BF16)
    grad_pre[...] = value
    shifted(value, g_cat)
    value = jnp.zeros((cells, chan), F32)
    for a in range(3):
        for b in range(3):
            piece = g_cat[pl.ds((2 - a) * COLS, cells), pl.ds((2 - b) * wide, wide)]
            value += dot_nt(piece, k_one[a, pl.ds(b * chan, chan)])
    grad_e[...] = value.astype(BF16)
    value = dot(h_cat[pl.ds(0, cells)], k_two[0])
    for tap in (1, 2):
        value += dot(h_cat[pl.ds(tap * COLS, cells)], k_two[tap])
    decoded[...] = value.astype(BF16)
    for colour in range(COLOURS):
        if colour < 2:
            source, cat, first, start, width = grad_pre, e_cat, COLS, 0, 3 * chan
            upstream = source[pl.ds(COLS, cells)]
        else:
            cat, first, start, width = h_cat, 0, 2, 3 * wide
            upstream = ext_c[pl.ds(2 * COLS, cells)]
        left[...] = dot_nt(permuted_rows(colour, wide), upstream).astype(BF16)
        at = 0
        for tap, low, high in segments(colour, start, width, span):
            found = dot(left[...], cat[pl.ds(first + tap * COLS, cells), pl.ds(low, high - low)])
            found = found.astype(BF16)
            terms[0, colour, :, pl.ds(at, high - low)] = found[: wide // 2]
            terms[1, colour, :, pl.ds(at, high - low)] = found[wide // 2 :]
            at += high - low


def local(ext_e, ext_c, kernel_one, kernel_two, cells):
    chan, wide = ext_e.shape[1], ext_c.shape[1]
    long, more = cells + 4 * COLS, cells + 2 * COLS
    span = 9 * (chan + wide) // COLOURS
    vmem = pl.BlockSpec(memory_space=pltpu.VMEM)
    return pl.pallas_call(
        local_kernel,
        out_shape=(
            jax.ShapeDtypeStruct((cells, wide), BF16),
            jax.ShapeDtypeStruct((cells, chan), BF16),
            jax.ShapeDtypeStruct((2, COLOURS, wide // 2, span), BF16),
        ),
        in_specs=[vmem] * 4,
        out_specs=(vmem,) * 3,
        scratch_shapes=[
            pltpu.VMEM((long, 3 * chan), BF16),
            pltpu.VMEM((long, 3 * wide), BF16),
            pltpu.VMEM((more, 3 * wide), BF16),
            pltpu.VMEM((more, 3 * wide), BF16),
            pltpu.VMEM((more, wide), F32),
            pltpu.VMEM((more, wide), BF16),
            pltpu.VMEM((wide, cells), BF16),
        ],
        name="local",
    )(ext_e, ext_c, kernel_one.reshape(3, 3 * chan, wide), kernel_two.reshape(3, 3 * wide, wide))


def back_kernel(
    w_hbm, grad_e, terms, book_out, kern_out,
    wbuf, gath, turned, table, whole, t_zero, t_snd, t_rcv, t_keep,
    r_zero, r_snd1, r_rcv1, r_keep1, r_snd2, r_rcv2, r_keep2, r_snd3, r_rcv3, r_keep3,
    r_snd4, r_rcv4, r_keep4, r_snd5, r_rcv5, r_keep5, r_snd6, r_rcv6, r_keep6,
    load_sem, send_sems, recv_sems,
):
    here = coords()
    core, z = here["core"], here["z"]
    partners, bits = links(here)
    twin = device(here, core=1 - core)
    cells, chan = grad_e.shape
    load = pltpu.make_async_copy(w_hbm, wbuf, load_sem)
    load.start()
    greet([twin] + partners)
    wire = Wire(send_sems, recv_sems)
    zu, zv = flip(z), 3 - z
    to_u, to_v = partners[4], partners[5]
    mid = cells // 2
    top, low = pl.ds(0, mid), pl.ds(mid, mid)

    a_u = wire.copy(grad_e.at[top], gath.at[z, 0], to_u)
    b_v = wire.copy(grad_e.at[low], gath.at[z, 1], to_v)
    zero = [wire.copy(terms.at[1 - core, k], r_zero.at[k], twin) for k in range(COLOURS)]
    a_v = wire.copy(grad_e.at[top], gath.at[z, 0], to_v)
    b_u = wire.copy(grad_e.at[low], gath.at[z, 1], to_u)

    rsnd = [None, r_snd1, r_snd2, r_snd3, r_snd4, r_snd5, r_snd6]
    rrcv = [None, r_rcv1, r_rcv2, r_rcv3, r_rcv4, r_rcv5, r_rcv6]
    rkeep = [None, r_keep1, r_keep2, r_keep3, r_keep4, r_keep5, r_keep6]
    moved = {}

    def reduce_step(k, step):
        dim = (k + step - 1) % 6
        bit, to = bits[dim], partners[dim]
        snd, keep = rsnd[step].at[k], rkeep[step].at[k]
        size = rsnd[step].shape[1]
        if step <= 4:
            if step == 1:
                zero[k].wait_recv()
                ours, theirs = terms.at[core, k], r_zero.at[k]
            else:
                moved[k].wait_recv()
                ours, theirs = rkeep[step - 1].at[k], rrcv[step - 1].at[k]

            def added(which):
                rows = pl.ds(pl.multiple_of(which * size, size), size)
                return (ours[rows].astype(F32) + theirs[rows].astype(F32)).astype(BF16)

            snd[...] = added(1 - bit)
            moved[k] = wire.copy(snd, rrcv[step].at[k], to)
            keep[...] = added(bit)
        else:
            moved[k].wait_recv()
            total = rkeep[step - 1][k].astype(F32) + rrcv[step - 1][k].astype(F32)
            upper, lower = total[:size], total[size:]
            snd[...] = jnp.where(bit == 0, lower, upper)
            moved[k] = wire.copy(snd, rrcv[step].at[k], to)
            keep[...] = jnp.where(bit == 0, upper, lower)

    def reduce_end(k):
        moved[k].wait_recv()
        kern_out[k] = r_keep6[k] + r_rcv6[k]

    for k in range(2):
        reduce_step(k, 1)
    a_u.wait_recv()
    a_far = wire.copy(gath.at[zu, 0], gath.at[zu, 0], to_v)
    b_v.wait_recv()
    b_far = wire.copy(gath.at[zv, 1], gath.at[zv, 1], to_u)
    for k in range(2, COLOURS):
        reduce_step(k, 1)

    gath[z, 0] = grad_e[top]
    gath[z, 1] = grad_e[low]
    row = lax.broadcasted_iota(jnp.int32, (chan, chan), 0)
    column = lax.broadcasted_iota(jnp.int32, (chan, chan), 1)
    unit = (row == column).astype(F32).astype(BF16)

    def turn(which, part):
        at = pl.multiple_of(which * cells + part * mid, mid)
        turned[:, pl.ds(at, mid)] = dot_nt(unit, gath[which, part]).astype(BF16)

    turn(z, 0)
    turn(z, 1)
    turn(zu, 0)
    turn(zv, 1)
    a_v.wait_recv()
    turn(zv, 0)
    b_u.wait_recv()
    turn(zu, 1)
    for k in range(COLOURS):
        reduce_step(k, 2)
    a_far.wait_recv()
    b_far.wait_recv()
    turn(rem(z + 2, 4), 0)
    turn(rem(z + 2, 4), 1)
    load.wait()
    codes = wbuf.shape[1]
    piece = codes // 8
    for n in range(8):
        part = dot(turned[...], wbuf[:, pl.ds(n * piece, piece)])
        table[n // 4, n % 4] = part.T.astype(BF16)

    t_first = [wire.copy(table.at[1 - core, k], t_zero.at[k], twin) for k in range(4)]
    hops = {}
    offsets = {}

    def table_step(k, step):
        dim = (k + step - 1) % 4
        bit, to = bits[dim], partners[dim]
        size = piece >> step
        at = pl.ds(piece - 2 * size, size)
        before = pl.ds(piece - 4 * size, 2 * size)
        if step == 1:
            t_first[k].wait_recv()
            ours, theirs = table.at[core, k], t_zero.at[k]
        else:
            hops[k].wait_recv()
            ours, theirs = t_keep.at[k, before], t_rcv.at[k, before]

        def added(which):
            rows = pl.ds(pl.multiple_of(which * size, size), size)
            return (ours[rows].astype(F32) + theirs[rows].astype(F32)).astype(BF16)

        t_snd[k, at] = added(1 - bit)
        hops[k] = wire.copy(t_snd.at[k, at], t_rcv.at[k, at], to)
        t_keep[k, at] = added(bit)
        offsets[k, step] = (offsets[k, step - 1] if step > 1 else 0) + bit * size

    def table_turn(k):
        hops[k].wait_recv()
        size = piece >> 4
        at = pl.ds(piece - 2 * size, size)
        rows = pl.ds(pl.multiple_of(offsets[k, 4], size), size)
        whole[core, k, rows] = (t_keep[k, at].astype(F32) + t_rcv[k, at].astype(F32)).astype(BF16)

    def table_gather(k, step):
        dim = (k + step - 1) % 4
        size = piece >> step
        if step < 4:
            hops[k].wait_recv()
        rows = pl.ds(pl.multiple_of(offsets[k, step], size), size)
        hops[k] = wire.copy(whole.at[core, k, rows], whole.at[core, k, rows], partners[dim])

    for k in range(4):
        table_step(k, 1)
    for k in range(COLOURS):
        reduce_step(k, 3)
    for k in range(4):
        table_step(k, 2)
    for k in range(COLOURS):
        reduce_step(k, 4)
    for k in range(4):
        table_step(k, 3)
    for k in range(COLOURS):
        reduce_step(k, 5)
    for k in range(4):
        table_step(k, 4)
    for k in range(COLOURS):
        reduce_step(k, 6)
    for k in range(4):
        table_turn(k)
        table_gather(k, 4)
    for k in range(COLOURS):
        reduce_end(k)
    for step in (3, 2, 1):
        for k in range(4):
            table_gather(k, step)
    ends = []
    for k in range(4):
        hops[k].wait_recv()
        ends.append(wire.copy(whole.at[core, k], whole.at[core, k], twin))
        book_out[core, k] = whole[core, k]
    for k in range(4):
        ends[k].wait_recv()
        book_out[1 - core, k] = whole[1 - core, k]
    wire.drain()


def back(weights, grad_e, terms):
    cells, chan = grad_e.shape
    codes = weights.shape[1]
    span, rows = terms.shape[3], terms.shape[2]
    piece = codes // 8
    vmem = pl.BlockSpec(memory_space=pltpu.VMEM)
    stages = []
    for step in range(1, 7):
        kind = BF16 if step <= 4 else F32
        stages += [pltpu.VMEM((COLOURS, rows >> step, span), kind)] * 3
    copies = 6 + COLOURS * 7 + 4 * 10
    return pl.pallas_call(
        back_kernel,
        out_shape=(
            jax.ShapeDtypeStruct((2, 4, piece, chan), BF16),
            jax.ShapeDtypeStruct((COLOURS, rows >> 6, span), F32),
        ),
        in_specs=[pl.BlockSpec(memory_space=pl.ANY), vmem, vmem],
        out_specs=(vmem, vmem),
        scratch_shapes=[
            pltpu.VMEM(weights.shape, BF16),
            pltpu.VMEM((4, 2, cells // 2, chan), BF16),
            pltpu.VMEM((chan, 4 * cells), BF16),
            pltpu.VMEM((2, 4, piece, chan), BF16),
            pltpu.VMEM((2, 4, piece, chan), BF16),
            pltpu.VMEM((4, piece, chan), BF16),
            pltpu.VMEM((4, piece, chan), BF16),
            pltpu.VMEM((4, piece, chan), BF16),
            pltpu.VMEM((4, piece, chan), BF16),
            pltpu.VMEM((COLOURS, rows, span), BF16),
            *stages,
            pltpu.SemaphoreType.DMA,
            pltpu.SemaphoreType.DMA((copies,)),
            pltpu.SemaphoreType.DMA((copies,)),
        ],
        compiler_params=pltpu.CompilerParams(collective_id=1, has_side_effects=True),
        name="back",
    )(weights, grad_e, terms)


def on_device(soft_weights, codebook, kernel_one, kernel_two, cotangent):
    own_rows, breadth, wide = cotangent.shape[1:]
    codes, chan = codebook.shape
    cells = own_rows * breadth
    weights = soft_weights.reshape(-1, codes)
    upstream = cotangent.reshape(cells, wide)
    ext_e, ext_c = front(weights, codebook, upstream)
    decoded, grad_e, terms = local(ext_e, ext_c, kernel_one, kernel_two, cells)
    book, kern = back(weights, grad_e, terms)

    def taps(part, depth):
        lines = part.transpose(1, 0, 2).reshape(part.shape[1], 3, 3, depth)
        return lines.transpose(1, 2, 3, 0)

    return (
        decoded.reshape(cotangent.shape),
        taps(kern[:2], chan),
        taps(kern[2:], wide),
        book.reshape(codes, chan).astype(F32),
    )


def solution(mesh):
    in_specs = (
        P("clip", "space", None, "code"),
        P("code", None),
        P(),
        P(),
        P("clip", ("space", "code"), None, None),
    )
    out_specs = (
        P("clip", ("space", "code"), None, None),
        P(None, None, None, ("space", "code", "clip")),
        P(None, None, None, ("space", "code", "clip")),
        P("code", None),
    )
    return jax.shard_map(
        on_device, mesh=mesh, in_specs=in_specs, out_specs=out_specs, check_vma=False
    )
```

time: 511 us -> 111 us (0.22)
  waiting for transfers between devices: 322 us -> 0 us
  Pallas kernels: 0 us -> 105 us
  matrix products: 49.1 us -> 0 us
  blocking collectives: 44.1 us -> 0 us
  local copies, waits for them, and re-layouts: 36.6 us -> 2.91 us
  starting transfers between devices: 27.9 us -> 0 us
  between operations: 14.6 us -> 0.65 us
  other arithmetic: 15.2 us -> 2.7 us
    unnamed x4 -> x0, waiting for transfers between devices: 224 us -> none
    pallas_call x0 -> x3, Pallas kernels: none -> 105 us  [the longest x1 58.9 us: back(): pl.pallas_call(back_kernel, out_shape=(jax.ShapeDtypeStruct((2, 4, piece,...]
    psum x1 -> x0, waiting for transfers between devices: 70.1 us -> none  [on_device(): lax.psum(code_terms.astype(jnp.bfloat16), ('space', 'clip'))]
    dot_general x56 -> x0, matrix products: 49.1 us -> none  [the longest x18 17.2 us: taps_forward(): jnp.dot(window, kernel[first, second], preferred_element_type=jnp.float32)]
    psum x1 -> x0, blocking collectives: 44.1 us -> none  [on_device(): summed = lax.psum(partial_value, 'code')]
    all_gather x1 -> x0, waiting for transfers between devices: 27.6 us -> none  [on_device(): piece = lax.all_gather(grad_embedded, 'code', axis=0, tiled=True)]
    ppermute x8 -> x0, starting transfers between devices: 27.6 us -> none  [the longest x4 19.9 us: with_halo(): lax.ppermute(lax.slice_in_dim(block, 0, width, axis=dim), axis, backward)]
    another operation x2 -> x0, local copies, waits for them, and re-layouts: 21.1 us -> none  [kernel_grad(): return jnp.stack(result)]
  transfers between devices with their start and end apart: 11 -> 0, of which waited for: 3 -> 0; matrix products, arithmetic and copies ran while one was open for 13% -> 0% of each run, Pallas kernels for 0% -> 0%
where the time goes in v1:
time: 111 us
  Pallas kernels  105 us (95%)
  local copies, waits for them, and re-layouts  2.91 us (3%)
  other arithmetic  2.7 us (2%)
    pallas_call x1, Pallas kernels, back(): pl.pallas_call(back_kernel, out_shape=(jax.ShapeDtypeStruct((2, 4, piece,...  58.9 us
    pallas_call x1, Pallas kernels, front(): pl.pallas_call(front_kernel, out_shape=(jax.ShapeDtypeStruct((long, chan)...  25 us
    pallas_call x1, Pallas kernels, local(): pl.pallas_call(local_kernel, out_shape=(jax.ShapeDtypeStruct((cells, wide...  20.9 us
    convert_element_type x1, other arithmetic, on_device(): book.reshape(codes, chan).astype(F32)  2.7 us

profile of v1, /device:TPU:1, one launch (start us, length us, event | category | flops | bytes accessed | tf_op | source)
XLA Modules:
  0.0 111.1 jit_solution(2108975356425962477)
XLA Ops:
  0.6 25.0 %front.1 = (bf16[640,256]{1,0:T(8,128)(2,1)}, bf16[640,512]{1,0:T(8,128)(2,1)}) custom-call(bf16[2048,2048]{1,0:T(8,128)(2,1)} %bitcast.18, bf16[2048,256]{1,0:T(8,128)(2,1)} %book.1, bf16[512,512]{1,0:T(8,128)(2,1)} %bitcast.22), custom_call_target="tpu_custom_call" | custom-call | tf_op jit(solution)/shard_map/front/pallas_call | solution.py:194
  25.6 20.9 %local.1 = (bf16[512,512]{1,0:T(8,128)(2,1)}, bf16[512,256]{1,0:T(8,128)(2,1)}, bf16[2,6,256,1152]{3,2,1,0:T(8,128)(2,1)}) custom-call(bf16[640,256]{1,0:T(8,128)(2,1)} %get-tuple-element.11.ext_e, bf16[640,512]{1,0:T(8,128)(2,1)} %get-tuple-element.12.ext_c, bf16[3,768,512]{2,1,0:T(8,128)(2,1)} %bitcast.21, bf16[3,1536,512]{2,1,0:T(8,128)(2,1)} %bitcast.20), custom_call_target="tpu_custom_call" | custom-call | tf_op jit(solution)/shard_map/local/pallas_call | solution.py:325
  46.5 58.9 %back.1 = (bf16[2,4,256,256]{3,2,1,0:T(8,128)(2,1)}, f32[6,4,1152]{2,1,0:T(4,128)}) custom-call(bf16[2048,2048]{1,0:T(8,128)(2,1)} %bitcast.19, bf16[512,256]{1,0:T(8,128)(2,1)} %get-tuple-element.14.grad_e, bf16[2,6,256,1152]{3,2,1,0:T(8,128)(2,1)} %get-tuple-element.15.terms), custom_call_target="tpu_custom_call" | custom-call | tf_op jit(solution)/shard_map/back/pallas_call | solution.py:538
  105.4 1.4 %slice.6 = f32[2,4,1152]{2,1,0:T(4,128)} slice(f32[6,4,1152]{2,1,0:T(4,128)} %get-tuple-element.16), slice={[0:2], [0:4], [0:1152]} | slice | bytes 73728 | tf_op jit(solution)/shard_map/slice | solution.py:583
  106.8 1.5 %slice.7 = f32[4,4,1152]{2,1,0:T(4,128)} slice(f32[6,4,1152]{2,1,0:T(4,128)} %get-tuple-element.16), slice={[2:6], [0:4], [0:1152]} | slice | bytes 147456 | tf_op jit(solution)/shard_map/slice | solution.py:584
  108.4 2.7 %bitcast_convert_fusion = f32[2048,256]{1,0:T(8,128)} fusion(bf16[2,4,256,256]{3,2,1,0:T(8,128)(2,1)} %get-tuple-element.17), kind=kLoop, calls=%fused_computation | loop fusion | flops 524288 | bytes 3145728 | tf_op jit(solution)/shard_map/convert_element_type | solution.py:585
